TPU v7x, 32 devices: a whole 2x2x4 slice. The times are simulated.
32 devices in a mesh: blk: 8 (over z, x), mp: 4 (over y, core).
Axes of the slice: x: 2, y: 2, z: 4, core: 2. Of those that a mesh axis runs over, the one named last changes fastest.
Arguments:
- lengths: int32 [4], replicated, may hold values from 1 to 512, 1024 in all
- groups: int32 [4], replicated, may hold values from 0 to 3, as said below
- deal: int32 [1024], P('blk'), may hold values from 0 to 1023, as said below
- prefix_block: int32 [8], P('blk'), may hold values from 0 to 7, each once
- queries: bfloat16 [1024, 2048], P('blk', 'mp'), may hold values from -8 to 8
- keys: bfloat16 [1024, 512], P('blk', 'mp'), may hold values from -8 to 8
- values: bfloat16 [1024, 512], P('blk', 'mp'), may hold values from -6 to 6
- prefix_key_blocks: bfloat16 [512, 512], P('blk', 'mp'), may hold values from -8 to 8
- prefix_value_blocks: bfloat16 [512, 512], P('blk', 'mp'), may hold values from -6 to 6
- out_weight: bfloat16 [2048, 4096], P('mp'), may hold values from -0.125 to 0.125
Outputs:
- layer_out: bfloat16 [1024, 4096], P('blk', 'mp')
Inputs may be any that keep to these rules, and one draw needn't show every extreme that they name: The 4 lengths sum to 1024; the largest is 512. `groups`: each group has exactly 1 request. `deal`: a permutation of the request-order rows; on every index of blk, the 16 slots c * 16 to c * 16 + 15 hold rows taken from request-order rows c * 128 to c * 128 + 127, and over all indices of blk each of those rows appears once. `prefix_block`: a permutation of the blocks.
All inputs are finite; a program needn't handle non-finite values.
Results may differ from a plain program's by a relative error of at most 0.012.
Values may be sent and summed in bfloat16 or wider, within the bound.
A program may use at most 64 MiB of HBM per device.

v0:
```python
import math

import jax
import jax.numpy as jnp
from jax import lax
from jax.sharding import PartitionSpec as P

HEAD_WIDTH = 128
GROUPS = 4


NEGATIVE = -1e30


def request_index(row_ids, req_ends):
    return jnp.sum((row_ids[:, None] >= req_ends[None, :]).astype(jnp.int32), axis=1)


def lookup(values_table, indices):
    slots = jnp.arange(values_table.shape[0], dtype=jnp.int32)
    return jnp.sum(jnp.where(indices[:, None] == slots[None, :], values_table[None, :], 0), axis=1)


def attend(flash_state, grouped, key_block, value_block, visible):
    run_best, run_total, run_accum = flash_state
    key_count = key_block.shape[0]
    kv_heads = grouped.shape[1]
    head_size = grouped.shape[3]
    score_scale = 1.0 / math.sqrt(head_size)
    keys_three = key_block.reshape(key_count, kv_heads, head_size)
    values_three = value_block.reshape(key_count, kv_heads, head_size)
    scores = (
        jnp.einsum("rgjd,ngd->rgjn", grouped, keys_three, preferred_element_type=jnp.float32)
        * score_scale
    )
    shown = visible[:, None, None, :]
    scores = jnp.where(shown, scores, NEGATIVE)
    new_best = jnp.maximum(run_best, jnp.max(scores, axis=3))
    weights = jnp.where(shown, jnp.exp(scores - new_best[..., None]), 0.0)
    factor = jnp.exp(run_best - new_best)
    run_total = run_total * factor + jnp.sum(weights, axis=3)
    mixed = jnp.einsum(
        "rgjn,ngd->rgjd",
        weights.astype(jnp.bfloat16),
        values_three,
        preferred_element_type=jnp.float32,
    )
    run_accum = run_accum * factor[..., None] + mixed
    return (new_best, run_total, run_accum)


def sweep(flash_state, grouped, key_block, value_block, key_info, visible_of):
    key_count = key_block.shape[0]
    step_width = key_count if key_count <= 1024 else math.gcd(key_count, 512)
    if step_width == key_count:
        return attend(flash_state, grouped, key_block, value_block, visible_of(key_info))

    def one_step(carried, step_index):
        offset = step_index * step_width
        key_part = lax.dynamic_slice_in_dim(key_block, offset, step_width, 0)
        value_part = lax.dynamic_slice_in_dim(value_block, offset, step_width, 0)
        info_part = lax.dynamic_slice_in_dim(key_info, offset, step_width, 0)
        return (attend(carried, grouped, key_part, value_part, visible_of(info_part)), None)

    flash_state, _ = lax.scan(
        one_step, flash_state, jnp.arange(key_count // step_width, dtype=jnp.int32)
    )
    return flash_state


def shards(
    lengths,
    groups,
    deal,
    prefix_block,
    queries,
    keys,
    values,
    prefix_key_blocks,
    prefix_value_blocks,
    out_weight,
):
    count_rows = queries.shape[0]
    kv_heads = keys.shape[1] // HEAD_WIDTH
    query_per_key_head = queries.shape[1] // keys.shape[1]
    devices = lax.axis_size("blk")
    my_index = lax.axis_index("blk")
    piece_rows = count_rows // devices
    per_group = devices // GROUPS
    prefix_rows = prefix_key_blocks.shape[0]
    req_ends = jnp.cumsum(lengths)
    arrived = lax.all_to_all(
        deal.reshape(devices, piece_rows), "blk", split_axis=0, concat_axis=0, tiled=True
    )
    placed = arrived.reshape(count_rows) - my_index * count_rows

    def prefix_pass(flash_state, grouped, query_group, block_ids):

        def prefix_step(carried, kv_piece):
            key_count = kv_piece[0].shape[0]
            owners = jnp.arange(key_count, dtype=jnp.int32) // prefix_rows
            key_group = jnp.take(block_ids, owners) // per_group

            def same_group(key_info):
                return key_info[None, :] == query_group[:, None]

            return sweep(carried, grouped, kv_piece[0], kv_piece[1], key_group, same_group)

        return prefix_step(
            flash_state,
            (
                lax.all_gather(prefix_key_blocks, "blk", axis=0, tiled=True),
                lax.all_gather(prefix_value_blocks, "blk", axis=0, tiled=True),
            ),
        )

    def suffix_rule(query_rows, query_req):

        def same_request(key_info):
            key_req = request_index(key_info, req_ends)
            return (
                (key_info[None, :] >= 0)
                & (key_req[None, :] == query_req[:, None])
                & (key_info[None, :] <= query_rows[:, None])
            )

        return same_request

    key_rows, block_ids = (
        lax.all_gather(deal, "blk", axis=0, tiled=True),
        lax.all_gather(prefix_block, "blk", axis=0, tiled=True),
    )
    query_rows = deal
    query_req = request_index(query_rows, req_ends)
    query_group = lookup(groups, query_req)
    grouped = queries.reshape(count_rows, kv_heads, query_per_key_head, HEAD_WIDTH)
    flash_state = prefix_pass(
        (
            jnp.full((count_rows, kv_heads, query_per_key_head), NEGATIVE, jnp.float32),
            jnp.zeros((count_rows, kv_heads, query_per_key_head), jnp.float32),
            jnp.zeros((count_rows, kv_heads, query_per_key_head, HEAD_WIDTH), jnp.float32),
        ),
        grouped,
        query_group,
        block_ids,
    )
    visible_of = suffix_rule(query_rows, query_req)
    kv_piece = (
        lax.all_gather(keys, "blk", axis=0, tiled=True),
        lax.all_gather(values, "blk", axis=0, tiled=True),
    )
    key_info = key_rows
    flash_state = sweep(flash_state, grouped, kv_piece[0], kv_piece[1], key_info, visible_of)
    run_best, run_total, run_accum = flash_state
    attended = (run_accum / run_total[..., None]).astype(jnp.bfloat16).reshape(count_rows, -1)
    returned = lax.all_to_all(
        attended.reshape(devices, piece_rows, -1), "blk", split_axis=0, concat_axis=0, tiled=True
    )
    flat = returned.reshape(count_rows, returned.shape[2])
    ordered = jnp.zeros_like(flat).at[placed].set(flat)
    partial_value = jnp.dot(ordered, out_weight, preferred_element_type=jnp.float32)
    return lax.psum_scatter(
        partial_value.astype(jnp.bfloat16), "mp", scatter_dimension=1, tiled=True
    )


def solution(mesh):
    return jax.shard_map(
        shards,
        mesh=mesh,
        in_specs=(
            P(),
            P(),
            P("blk"),
            P("blk"),
            P("blk", "mp"),
            P("blk", "mp"),
            P("blk", "mp"),
            P("blk", "mp"),
            P("blk", "mp"),
            P("mp", None),
        ),
        out_specs=P("blk", "mp"),
        check_vma=False,
    )
```

profile of v0, /device:TPU:0, one launch (start us, length us, event | category | flops | bytes accessed | tf_op | source)
XLA Modules:
  0.0 230.1 jit_solution(1636237273558272072)
XLA Ops:
  6.5 1.4 all_to_all.9
  7.9 7.3 %all-to-all-start = ((s32[8,1,16]{2,1,0:T(1,128)}), s32[8,1,16]{2,1,0:T(1,128)S(1)}, u32[]{:S(2)}, u32[]{:S(2)}) async-start(s32[8,1,16]{2,1,0:T(1,128)} %bitcast), calls=%async_computation | async-start | bytes 8192 | tf_op jit(solution)/shard_map/all_to_all | solution.py:92
  15.2 0.8 reduce-window.8
  16.0 0.7 convert_reduce_fusion.1
  16.7 21.0 %all-gather = s32[8,1,128]{2,1,0:T(1,128)S(1)} all-gather(s32[1,1,128]{2,1,0:T(1,128)} %bitcast.108), channel_id=1, replica_groups=mesh['blk'=8,'mp'=4] {'blk'}, dimensions={0}, use_global_device_ids=true | all-gather | bytes 4608 | tf_op jit(solution)/shard_map/all_gather | solution.py:130
  38.5 1.2 dynamic-slice
  39.7 0.8 dynamic-update-slice
  40.5 6.8 %all-reduce = s32[8]{0:T(128)S(1)} all-reduce(s32[8]{0:T(128)S(1)} %dynamic-update-slice), channel_id=1, replica_groups=mesh['blk'=8,'mp'=4] {'blk'}, use_global_device_ids=true, to_apply=%add | all-reduce | flops 8 | bytes 64
  47.3 0.7 fusion.47
  48.0 32.5 %all_gather.19 = bf16[512,128]{1,0:T(8,128)(2,1)S(1)} all-gather(bf16[64,128]{1,0:T(8,128)(2,1)} %param.17), channel_id=1, replica_groups=mesh['blk'=8,'mp'=4] {'blk'}, dimensions={0}, use_global_device_ids=true | all-gather | bytes 147456 | tf_op jit(solution)/shard_map/all_gather | solution.py:112
  80.5 30.9 %all_gather.22 = bf16[1024,128]{1,0:T(8,128)(2,1)S(1)} all-gather(bf16[128,128]{1,0:T(8,128)(2,1)} %param.15), channel_id=1, replica_groups=mesh['blk'=8,'mp'=4] {'blk'}, dimensions={0}, use_global_device_ids=true | all-gather | bytes 294912 | tf_op jit(solution)/shard_map/all_gather | solution.py:149
  111.5 31.0 %all_gather.23 = bf16[1024,128]{1,0:T(8,128)(2,1)S(1)} all-gather(bf16[128,128]{1,0:T(8,128)(2,1)} %param.16), channel_id=1, replica_groups=mesh['blk'=8,'mp'=4] {'blk'}, dimensions={0}, use_global_device_ids=true | all-gather | bytes 294912 | tf_op jit(solution)/shard_map/all_gather | solution.py:150
  142.5 0.7 select_reduce_fusion
  143.2 4.3 %compare_select_fusion.1 = s32[512,1]{0,1:T(1,128)S(1)} fusion(s32[]{:T(128)} %bitcast.4, s32[]{:T(128)} %bitcast.5, s32[]{:T(128)} %bitcast.6, s32[]{:T(128)} %bitcast.7, s32[]{:T(128)} %bitcast.8, s32[]{:T(128)} %bitcast.10, s32[]{:T(128)} %bitcast.9), kind=kLoop, calls=%fused_computation.47 | loop fusion | flops 11776 | bytes 2076 | tf_op jit(solution)/shard_map/jit(_take)/gather | solution.py:102
  147.6 0.7 add_select_fusion
  148.4 1.5 compare_and_fusion
  151.3 0.8 convolution_bitcast_fusion.1
  152.0 30.5 %all_gather.20 = bf16[512,128]{1,0:T(8,128)(2,1)S(1)} all-gather(bf16[64,128]{1,0:T(8,128)(2,1)S(1)} %copy-done.1), channel_id=1, replica_groups=mesh['blk'=8,'mp'=4] {'blk'}, dimensions={0}, use_global_device_ids=true | all-gather | bytes 147456 | tf_op jit(solution)/shard_map/all_gather | solution.py:113
  183.4 0.7 reshape_reshape.3
  184.1 4.0 %all-to-all-start.1 = ((bf16[8,16,512]{2,1,0:T(8,128)(2,1)}), bf16[8,16,512]{2,1,0:T(8,128)(2,1)S(1)}, u32[]{:S(2)}, u32[]{:S(2)}) async-start(bf16[8,16,512]{2,1,0:T(8,128)(2,1)} %reshape_reshape.3), calls=%async_computation.1 | async-start | bytes 262144 | tf_op jit(solution)/shard_map/all_to_all | solution.py:156
  188.2 7.2 %all-to-all-done.1 = bf16[8,16,512]{2,1,0:T(8,128)(2,1)S(1)} async-done(((bf16[8,16,512]{2,1,0:T(8,128)(2,1)}), bf16[8,16,512]{2,1,0:T(8,128)(2,1)S(1)}, u32[]{:S(2)}, u32[]{:S(2)}) %all-to-all-start.1) | async-done | bytes 131104 | tf_op jit(solution)/shard_map/all_to_all | solution.py:156
  195.4 1.1 scatter_custom_fusion
  196.5 3.9 %convolution_convert_fusion = bf16[128,4096]{1,0:T(8,128)(2,1)} fusion(bf16[128,512]{1,0:T(8,128)(2,1)S(1)} %scatter_custom_fusion, bf16[512,4096]{1,0:T(8,128)(2,1)} %param.19), kind=kOutput, calls=%fused_computation.1 | convolution fusion | flops 537395200 | bytes 5373952 | tf_op jit(solution)/shard_map/dot_general | solution.py:161
  200.4 22.9 %reduce-scatter.2.cloned.1.call-done = bf16[128,1024]{1,0:T(8,128)(2,1)} async-done(((bf16[128,4096]{1,0:T(8,128)(2,1)}), bf16[128,1024]{1,0:T(8,128)(2,1)}) %reduce-scatter.2.cloned.1.call-update) | async-done | bytes 262160 | tf_op jit(solution)/shard_map/reduce_scatter | solution.py:162
  (23 shorter events, 2.5 us)
Async XLA Ops:
  6.5 143.4 %copy-start = (bf16[128,512]{1,0:T(8,128)(2,1)S(1)}, bf16[128,512]{1,0:T(8,128)(2,1)}, u32[]{:S(2)}) copy-start(bf16[128,512]{1,0:T(8,128)(2,1)} %param.14) | copy-start | bytes 393220
  7.9 176.2 %all-to-all-start = ((s32[8,1,16]{2,1,0:T(1,128)}), s32[8,1,16]{2,1,0:T(1,128)S(1)}, u32[]{:S(2)}, u32[]{:S(2)}) async-start(s32[8,1,16]{2,1,0:T(1,128)} %bitcast), calls=%async_computation | async-start | bytes 8192 | tf_op jit(solution)/shard_map/all_to_all | solution.py:92
  151.2 0.8 copy-start.1
  184.1 11.3 %all-to-all-start.1 = ((bf16[8,16,512]{2,1,0:T(8,128)(2,1)}), bf16[8,16,512]{2,1,0:T(8,128)(2,1)S(1)}, u32[]{:S(2)}, u32[]{:S(2)}) async-start(bf16[8,16,512]{2,1,0:T(8,128)(2,1)} %reshape_reshape.3), calls=%async_computation.1 | async-start | bytes 262144 | tf_op jit(solution)/shard_map/all_to_all | solution.py:156
  188.1 35.2 %reduce-scatter.2.cloned.1.call-start = ((), (), s32[]{:S(2)}) async-start(), calls=%async_computation.3 | async-start | bytes 1310720 | tf_op jit(solution)/shard_map/reduce_scatter | solution.py:162
Sparse Core Ops, SparseCore 0:
  200.5 22.6 reduce-scatter.1
where the time goes:
time: 231 us; the launch traced here: 230 us
  blocking collectives  153 us (66%)
  waiting for transfers between devices  30.1 us (13%)
  between operations  14.2 us (6%)
  starting transfers between devices  11.3 us (5%)
  other arithmetic  9.85 us (4%)
  local copies, waits for them, and re-layouts  6.03 us (3%)
  matrix products  5.89 us (3%)
    all_gather x1, blocking collectives, prefix_pass(): lax.all_gather(prefix_key_blocks, 'blk', axis=0, tiled=True)  32.5 us
    all_gather x1, blocking collectives, shards(): lax.all_gather(values, 'blk', axis=0, tiled=True)  31 us
    all_gather x1, blocking collectives, shards(): lax.all_gather(keys, 'blk', axis=0, tiled=True)  30.9 us
    all_gather x1, blocking collectives, prefix_pass(): lax.all_gather(prefix_value_blocks, 'blk', axis=0, tiled=True)  30.5 us
    reduce_scatter x1, waiting for transfers between devices, shards(): lax.psum_scatter(partial_value.astype(jnp.bfloat16), 'mp', scatter_dimens...  22.9 us
    all_gather x1, blocking collectives, shards(): lax.all_gather(deal, 'blk', axis=0, tiled=True)  21 us
    all_to_all x1, starting transfers between devices, shards(): lax.all_to_all(deal.reshape(devices, piece_rows), 'blk', split_axis=0, co...  7.25 us
    all_to_all x1, waiting for transfers between devices, shards(): lax.all_to_all(attended.reshape(devices, piece_rows, -1), 'blk', split_ax...  7.19 us
  transfers between devices with their start and end apart: 3, of which 2 were waited for; matrix products, arithmetic and copies ran while one was open for 7% of the time, Pallas kernels for 0%

commit v1 on v0

--- a/solution.py
+++ b/solution.py
@@ -1,8 +1,11 @@
+import functools
 import math
 
 import jax
 import jax.numpy as jnp
 from jax import lax
+from jax.experimental import pallas as pl
+from jax.experimental.pallas import tpu as pltpu
 from jax.sharding import PartitionSpec as P
 
 HEAD_WIDTH = 128
@@ -68,7 +71,7 @@
     return flash_state
 
 
-def shards(
+def plain_shards(
     lengths,
     groups,
     deal,
@@ -164,6 +167,365 @@
     )
 
 
+LOG2E = 1.4426950408889634
+
+
+def fused_kernel(
+    devices,
+    lengths_ref,
+    groups_ref,
+    block_ref,
+    deal_ref,
+    q_hbm,
+    k_hbm,
+    v_hbm,
+    pk_hbm,
+    pv_hbm,
+    w_hbm,
+    out_ref,
+    q_buf,
+    k_buf,
+    v_buf,
+    pk_buf,
+    pv_buf,
+    w_buf,
+    meta_buf,
+    score_buf,
+    weight_buf,
+    top_buf,
+    bias_buf,
+    att_buf,
+    ret_buf,
+    send_a,
+    recv_a,
+    send_b,
+    recv_b,
+    send_c,
+    recv_c,
+    part_buf,
+    local_sem,
+    own_sem,
+    w_sem,
+    gather_send,
+    gather_recv,
+    a2a_send,
+    a2a_recv,
+    red_send,
+    red_recv,
+):
+    n = devices
+    me = lax.axis_index("blk")
+    m = lax.axis_index("mp")
+    y = m // 2
+    c = m - y * 2
+    sibling = y * 2 + (1 - c)
+    across = (1 - y) * 2 + c
+    rows = q_buf.shape[0]
+    heads = q_buf.shape[1] // HEAD_WIDTH
+    piece = rows // n
+    requests = lengths_ref.shape[0]
+    per_group = n // GROUPS
+    width = out_ref.shape[1]
+    peers = [lax.rem(me + k, n) for k in range(n)]
+    MESH = pl.DeviceIdType.MESH
+
+    meta_buf[0] = jnp.zeros(meta_buf.shape[1:], jnp.int32)
+    meta_buf[0, 0:1, :] = deal_ref[...]
+    meta_buf[0, 1:2, :] = jnp.full((1, rows), block_ref[0] // per_group, jnp.int32)
+
+    barrier = pltpu.get_barrier_semaphore()
+    for k in range(1, n):
+        pl.semaphore_signal(barrier, inc=1, device_id={"blk": peers[k]}, device_id_type=MESH)
+    pl.semaphore_signal(barrier, inc=1, device_id={"mp": sibling}, device_id_type=MESH)
+    pl.semaphore_signal(barrier, inc=1, device_id={"mp": across}, device_id_type=MESH)
+
+    local = [
+        pltpu.make_async_copy(q_hbm, q_buf, local_sem.at[0]),
+        pltpu.make_async_copy(k_hbm, k_buf.at[0], local_sem.at[1]),
+        pltpu.make_async_copy(v_hbm, v_buf.at[0], local_sem.at[2]),
+        pltpu.make_async_copy(pk_hbm, pk_buf.at[0], local_sem.at[3]),
+        pltpu.make_async_copy(pv_hbm, pv_buf.at[0], local_sem.at[4]),
+    ]
+    for copy in local:
+        copy.start()
+    order = [across_col for across_col in ((1 - y) * 2 + (1 - c), across, sibling, m)]
+    w_copies = [
+        pltpu.make_async_copy(
+            w_hbm.at[:, pl.ds(pl.multiple_of(order[i] * width, 128), width)],
+            w_buf.at[i],
+            w_sem.at[i],
+        )
+        for i in range(4)
+    ]
+    for copy in w_copies:
+        copy.start()
+    pl.semaphore_wait(barrier, n + 1)
+
+    def gather(k):
+        pairs = (
+            (meta_buf.at[0], meta_buf.at[k]),
+            (k_hbm, k_buf.at[k]),
+            (pk_hbm, pk_buf.at[k]),
+            (v_hbm, v_buf.at[k]),
+            (pv_hbm, pv_buf.at[k]),
+        )
+        return [
+            pltpu.make_async_remote_copy(
+                src_ref=source,
+                dst_ref=target,
+                send_sem=gather_send.at[k, i],
+                recv_sem=gather_recv.at[k, i],
+                device_id={"blk": peers[k]},
+                device_id_type=MESH,
+            )
+            for i, (source, target) in enumerate(pairs)
+        ]
+
+    gathers = [None] + [gather(k) for k in range(1, n)]
+    for i in range(5):
+        for k in range(1, n):
+            gathers[k][i].start()
+
+    def column(row):
+        return jnp.transpose(jnp.broadcast_to(row, (rows, rows)))
+
+    query_row = deal_ref[...]
+    start_row = jnp.zeros((1, rows), jnp.int32)
+    group_row = jnp.full((1, rows), groups_ref[0], jnp.int32)
+    end = lengths_ref[0]
+    for r in range(1, requests):
+        past = query_row >= end
+        start_row = jnp.where(past, end, start_row)
+        group_row = jnp.where(past, groups_ref[r], group_row)
+        end = end + lengths_ref[r]
+    row_col = column(query_row)
+    start_col = column(start_row)
+    group_col = column(group_row)
+
+    for copy in local:
+        copy.wait()
+    scale = LOG2E / math.sqrt(HEAD_WIDTH)
+
+    def scored(h, keys, bias):
+        return (
+            lax.dot_general(
+                q_buf[:, h * HEAD_WIDTH : (h + 1) * HEAD_WIDTH],
+                keys,
+                (((1,), (1,)), ((), ())),
+                preferred_element_type=jnp.float32,
+            )
+            * scale
+            + bias
+        )
+
+    def place(block, keys, bias, first):
+        for h in range(heads):
+            scores = scored(h, keys, bias)
+            score_buf[block, h] = scores
+            if first:
+                top_buf[h] = scores
+            else:
+                top_buf[h] = jnp.maximum(top_buf[h], scores)
+
+    lane = lax.broadcasted_iota(jnp.int32, (1, rows), 1)
+    for k in range(n):
+        if k > 0:
+            gathers[k][0].wait_recv()
+            gathers[k][1].wait_recv()
+        key_row = meta_buf[k, 0:1, :]
+        shown = (key_row >= start_col) & (key_row <= row_col)
+        bias = jnp.where(shown, 0.0, NEGATIVE)
+        place(k, k_buf[k], bias, k == 0)
+    for k in range(0, n, 2):
+        for j in (k, k + 1):
+            if j > 0:
+                gathers[j][2].wait_recv()
+        key_group = jnp.where(lane < rows // 2, meta_buf[k, 1:2, :], meta_buf[k + 1, 1:2, :])
+        bias = jnp.where(key_group == group_col, 0.0, NEGATIVE)
+        place(n + k // 2, pk_buf[k : k + 2].reshape(rows, HEAD_WIDTH), bias, False)
+
+    blocks = n + n // 2
+    totals = []
+    for h in range(heads):
+        top = jnp.max(top_buf[h], axis=1, keepdims=True)
+        total = jnp.zeros((rows, rows), jnp.float32)
+        for b in range(blocks):
+            weights = jnp.exp2(score_buf[b, h] - top)
+            total = total + weights
+            weight_buf[h * rows : (h + 1) * rows, b * rows : (b + 1) * rows] = weights.astype(
+                jnp.bfloat16
+            )
+        totals.append(jnp.sum(total, axis=1, keepdims=True))
+    for k in range(1, n):
+        gathers[k][3].wait_recv()
+        gathers[k][4].wait_recv()
+    mixed = jnp.dot(
+        weight_buf[:, : n * rows],
+        v_buf[...].reshape(n * rows, HEAD_WIDTH),
+        preferred_element_type=jnp.float32,
+    ) + jnp.dot(
+        weight_buf[:, n * rows :],
+        pv_buf[...].reshape(n * rows // 2, HEAD_WIDTH),
+        preferred_element_type=jnp.float32,
+    )
+    for h in range(heads):
+        done = (mixed[h * rows : (h + 1) * rows] / totals[h]).astype(jnp.bfloat16)
+        att_buf[:, :, h * HEAD_WIDTH : (h + 1) * HEAD_WIDTH] = done.reshape(n, piece, HEAD_WIDTH)
+
+    returns = [None] + [
+        pltpu.make_async_remote_copy(
+            src_ref=att_buf.at[peers[k]],
+            dst_ref=ret_buf.at[k],
+            send_sem=a2a_send.at[k],
+            recv_sem=a2a_recv.at[k],
+            device_id={"blk": peers[k]},
+            device_id_type=MESH,
+        )
+        for k in range(1, n)
+    ]
+    for k in range(1, n):
+        returns[k].start()
+    ret_buf[0:1] = att_buf[pl.ds(me, 1)]
+
+    placed = jnp.zeros((1, rows), jnp.int32)
+    for k in range(n):
+        shift = lax.rem((k + n - me) * piece, rows)
+        turned = pltpu.roll(meta_buf[k], shift, 1)[0:1, :]
+        placed = jnp.where((lane >= k * piece) & (lane < (k + 1) * piece), turned, placed)
+    placed = placed - me * rows
+    target = lax.broadcasted_iota(jnp.int32, (rows, rows), 0)
+    select = jnp.where(target == placed, 1.0, 0.0).astype(jnp.bfloat16)
+    for k in range(1, n):
+        returns[k].wait_recv()
+    ordered = jnp.dot(
+        select, ret_buf[...].reshape(rows, -1), preferred_element_type=jnp.float32
+    ).astype(jnp.bfloat16)
+
+    def reduce_copy(i, source, target, device):
+        return pltpu.make_async_remote_copy(
+            src_ref=source,
+            dst_ref=target,
+            send_sem=red_send.at[i],
+            recv_sem=red_recv.at[i],
+            device_id={"mp": device},
+            device_id_type=MESH,
+        )
+
+    def project(i):
+        w_copies[i].wait()
+        return jnp.dot(ordered, w_buf[i], preferred_element_type=jnp.float32)
+
+    copy_a = reduce_copy(0, send_a, recv_a, sibling)
+    copy_b = reduce_copy(1, send_b, recv_b, across)
+    copy_c = reduce_copy(2, send_c, recv_c, sibling)
+    send_a[...] = project(0).astype(jnp.bfloat16)
+    copy_a.start()
+    part_buf[...] = project(1)
+    copy_a.wait_recv()
+    send_b[...] = (part_buf[...] + recv_a[...].astype(jnp.float32)).astype(jnp.bfloat16)
+    copy_b.start()
+    send_c[...] = project(2).astype(jnp.bfloat16)
+    copy_c.start()
+    part_buf[...] = project(3)
+    copy_c.wait_recv()
+    part_buf[...] = part_buf[...] + recv_c[...].astype(jnp.float32)
+    copy_b.wait_recv()
+    out_ref[...] = (part_buf[...] + recv_b[...].astype(jnp.float32)).astype(jnp.bfloat16)
+    for k in range(1, n):
+        for copy in gathers[k]:
+            copy.wait_send()
+        returns[k].wait_send()
+    for copy in (copy_a, copy_b, copy_c):
+        copy.wait_send()
+
+
+def shards(
+    lengths,
+    groups,
+    deal,
+    prefix_block,
+    queries,
+    keys,
+    values,
+    prefix_key_blocks,
+    prefix_value_blocks,
+    out_weight,
+):
+    n = lax.axis_size("blk")
+    rows = queries.shape[0]
+    piece = rows // n
+    if piece % 16 != 0 or rows != 128 or 2 * prefix_key_blocks.shape[0] != rows:
+        return plain_shards(
+            lengths,
+            groups,
+            deal,
+            prefix_block,
+            queries,
+            keys,
+            values,
+            prefix_key_blocks,
+            prefix_value_blocks,
+            out_weight,
+        )
+    heads = queries.shape[1] // HEAD_WIDTH
+    prefix_rows = prefix_key_blocks.shape[0]
+    columns = out_weight.shape[1] // lax.axis_size("mp")
+    blocks = n + n // 2
+    bf16, f32 = jnp.bfloat16, jnp.float32
+    smem = pl.BlockSpec(memory_space=pltpu.SMEM)
+    vmem = pl.BlockSpec(memory_space=pltpu.VMEM)
+    hbm = pl.BlockSpec(memory_space=pl.ANY)
+    dma = pltpu.SemaphoreType.DMA
+    return pl.pallas_call(
+        functools.partial(fused_kernel, n),
+        out_shape=jax.ShapeDtypeStruct((rows, columns), bf16),
+        in_specs=[smem, smem, smem, vmem, hbm, hbm, hbm, hbm, hbm, hbm],
+        out_specs=vmem,
+        scratch_shapes=[
+            pltpu.VMEM((rows, queries.shape[1]), bf16),
+            pltpu.VMEM((n, rows, HEAD_WIDTH), bf16),
+            pltpu.VMEM((n, rows, HEAD_WIDTH), bf16),
+            pltpu.VMEM((n, prefix_rows, HEAD_WIDTH), bf16),
+            pltpu.VMEM((n, prefix_rows, HEAD_WIDTH), bf16),
+            pltpu.VMEM((4, out_weight.shape[0], columns), bf16),
+            pltpu.VMEM((n, 8, rows), jnp.int32),
+            pltpu.VMEM((blocks, heads, rows, rows), f32),
+            pltpu.VMEM((heads * rows, blocks * rows), bf16),
+            pltpu.VMEM((heads, rows, rows), f32),
+            pltpu.VMEM((rows, rows), f32),
+            pltpu.VMEM((n, piece, heads * HEAD_WIDTH), bf16),
+            pltpu.VMEM((n, piece, heads * HEAD_WIDTH), bf16),
+        ]
+        + [pltpu.VMEM((rows, columns), bf16)] * 6
+        + [
+            pltpu.VMEM((rows, columns), f32),
+            dma((5,)),
+            dma((1,)),
+            dma((4,)),
+            dma((n, 5)),
+            dma((n, 5)),
+            dma((n,)),
+            dma((n,)),
+            dma((3,)),
+            dma((3,)),
+        ],
+        compiler_params=pltpu.CompilerParams(
+            collective_id=0, has_side_effects=True, vmem_limit_bytes=40 << 20
+        ),
+    )(
+        lengths,
+        groups,
+        prefix_block,
+        deal.reshape(1, rows),
+        queries,
+        keys,
+        values,
+        prefix_key_blocks,
+        prefix_value_blocks,
+        out_weight,
+    )
+
+
 def solution(mesh):
     return jax.shard_map(
         shards,

time: 231 us -> 51.4 us (0.22)
  blocking collectives: 153 us -> 0 us
  Pallas kernels: 0 us -> 41.6 us
  waiting for transfers between devices: 30.1 us -> 0 us
  between operations: 14.2 us -> 0.68 us
  starting transfers between devices: 11.3 us -> 0 us
  other arithmetic: 9.85 us -> 0 us
  matrix products: 5.89 us -> 0 us
  local copies, waits for them, and re-layouts: 6.03 us -> 8.7 us
    all_gather x5 -> x0, blocking collectives: 146 us -> none  [the longest x1 32.5 us: prefix_pass(): lax.all_gather(prefix_key_blocks, 'blk', axis=0, tiled=True)]
    pallas_call x0 -> x1, Pallas kernels: none -> 41.6 us  [shards(): pl.pallas_call(functools.partial(fused_kernel, n), out_shape=jax.ShapeDty...]
    reduce_scatter x1 -> x0, waiting for transfers between devices: 22.9 us -> none  [shards(): lax.psum_scatter(partial_value.astype(jnp.bfloat16), 'mp', scatter_dimens...]
    all_to_all x2 -> x0, starting transfers between devices: 11.2 us -> none  [the longest x1 7.25 us: shards(): lax.all_to_all(deal.reshape(devices, piece_rows), 'blk', split_axis=0, co...]
    all_to_all x2 -> x0, waiting for transfers between devices: 7.19 us -> none  [the longest x1 7.19 us: shards(): lax.all_to_all(attended.reshape(devices, piece_rows, -1), 'blk', split_ax...]
    unnamed x1 -> x0, blocking collectives: 6.78 us -> none
    unnamed x7 -> x19, local copies, waits for them, and re-layouts: 2.01 us -> 8.7 us
    dot_general x5 -> x0, matrix products: 5.89 us -> none  [the longest x1 3.9 us: shards(): jnp.dot(ordered, out_weight, preferred_element_type=jnp.float32)]
  transfers between devices with their start and end apart: 3 -> 0, of which waited for: 2 -> 0; matrix products, arithmetic and copies ran while one was open for 7% -> 0% of each run, Pallas kernels for 0% -> 0%
where the time goes in v1:
time: 51.4 us; the launch traced here: 51 us
  Pallas kernels  41.6 us (81%)
  local copies, waits for them, and re-layouts  8.7 us (17%)
  between operations  0.68 us (1%)
    pallas_call x1, Pallas kernels, shards(): pl.pallas_call(functools.partial(fused_kernel, n), out_shape=jax.ShapeDty...  41.6 us
    unnamed x19, local copies, waits for them, and re-layouts  8.7 us

profile of v1, /device:TPU:0, one launch (start us, length us, event | category | flops | bytes accessed | tf_op | source)
XLA Modules:
  0.0 51.0 jit_solution(12061593551582436138)
XLA Ops:
  0.7 0.0 copy-start
  0.7 2.2 %copy-done = bf16[512,4096]{1,0:T(8,128)(2,1)S(1)} copy-done((bf16[512,4096]{1,0:T(8,128)(2,1)S(1)}, bf16[512,4096]{1,0:T(8,128)(2,1)}, u32[]{:S(2)}) %copy-start) | copy-done | bytes 4194328
  2.8 0.0 copy-start.1
  2.8 0.9 %copy-done.1 = bf16[128,512]{1,0:T(8,128)(2,1)S(1)} copy-done((bf16[128,512]{1,0:T(8,128)(2,1)S(1)}, bf16[128,512]{1,0:T(8,128)(2,1)}, u32[]{:S(2)}) %copy-start.1) | copy-done | bytes 131096
  3.7 0.0 copy-start.2
  3.7 0.8 %copy-done.2 = bf16[128,128]{1,0:T(8,128)(2,1)S(1)} copy-done((bf16[128,128]{1,0:T(8,128)(2,1)S(1)}, bf16[128,128]{1,0:T(8,128)(2,1)}, u32[]{:S(2)}) %copy-start.2) | copy-done | bytes 32792
  4.5 0.0 copy-start.3
  4.5 0.8 %copy-done.3 = bf16[128,128]{1,0:T(8,128)(2,1)S(1)} copy-done((bf16[128,128]{1,0:T(8,128)(2,1)S(1)}, bf16[128,128]{1,0:T(8,128)(2,1)}, u32[]{:S(2)}) %copy-start.3) | copy-done | bytes 32792
  5.3 0.0 copy-start.4
  5.3 0.7 %copy-done.4 = bf16[64,128]{1,0:T(8,128)(2,1)S(1)} copy-done((bf16[64,128]{1,0:T(8,128)(2,1)S(1)}, bf16[64,128]{1,0:T(8,128)(2,1)}, u32[]{:S(2)}) %copy-start.4) | copy-done | bytes 16408
  6.0 0.0 copy-start.5
  6.0 0.7 %copy-done.5 = bf16[64,128]{1,0:T(8,128)(2,1)S(1)} copy-done((bf16[64,128]{1,0:T(8,128)(2,1)S(1)}, bf16[64,128]{1,0:T(8,128)(2,1)}, u32[]{:S(2)}) %copy-start.5) | copy-done | bytes 16408
  6.7 0.0 copy-start.6
  6.7 0.7 %copy-done.6 = s32[4]{0:T(128)S(1)} copy-done((s32[4]{0:T(128)S(1)}, s32[4]{0:T(128)}, u32[]{:S(2)}) %copy-start.6) | copy-done | bytes 40
  7.4 0.0 copy-start.7
  7.4 0.7 %copy-done.7 = s32[4]{0:T(128)S(1)} copy-done((s32[4]{0:T(128)S(1)}, s32[4]{0:T(128)}, u32[]{:S(2)}) %copy-start.7) | copy-done | bytes 40
  8.0 0.0 copy-start.8
  8.0 0.7 %copy-done.8 = s32[128]{0:T(128)S(1)} copy-done((s32[128]{0:T(128)S(1)}, s32[128]{0:T(128)}, u32[]{:S(2)}) %copy-start.8) | copy-done | bytes 536
  8.7 41.6 %shard_map.100 = bf16[128,1024]{1,0:T(8,128)(2,1)S(1)} custom-call(s32[4]{0:T(128)S(1)} %copy-done.6, s32[4]{0:T(128)S(1)} %copy-done.7, s32[1]{0:T(128)S(6)} %copy.12.block_ref, s32[1,128]{1,0:T(1,128)S(1)} %bitcast.1, bf16[128,512]{1,0:T(8,128)(2,1)S(1)} %copy-done.1, bf16[128,128]{1,0:T(8,128)(2,1)S(1)} %copy-done.2, bf16[128,128]{1,0:T(8,128)(2,1)S(1)} %copy-done.3, ...), custom_call_target="tpu_custom_call" | custom-call | tf_op jit(solution)/shard_map/pallas_call | solution.py:479
  50.3 0.7 %copy.13 = bf16[128,1024]{1,0:T(8,128)(2,1)} copy(bf16[128,1024]{1,0:T(8,128)(2,1)S(1)} %shard_map.100) | data formatting | bytes 524288
Async XLA Ops:
  0.7 2.2 %copy-start = (bf16[512,4096]{1,0:T(8,128)(2,1)S(1)}, bf16[512,4096]{1,0:T(8,128)(2,1)}, u32[]{:S(2)}) copy-start(bf16[512,4096]{1,0:T(8,128)(2,1)} %w_hbm.1) | copy-start | bytes 12582916
  2.8 0.9 %copy-start.1 = (bf16[128,512]{1,0:T(8,128)(2,1)S(1)}, bf16[128,512]{1,0:T(8,128)(2,1)}, u32[]{:S(2)}) copy-start(bf16[128,512]{1,0:T(8,128)(2,1)} %q_hbm.1) | copy-start | bytes 393220
  3.7 0.8 %copy-start.2 = (bf16[128,128]{1,0:T(8,128)(2,1)S(1)}, bf16[128,128]{1,0:T(8,128)(2,1)}, u32[]{:S(2)}) copy-start(bf16[128,128]{1,0:T(8,128)(2,1)} %k_hbm.1) | copy-start | bytes 98308
  4.5 0.8 %copy-start.3 = (bf16[128,128]{1,0:T(8,128)(2,1)S(1)}, bf16[128,128]{1,0:T(8,128)(2,1)}, u32[]{:S(2)}) copy-start(bf16[128,128]{1,0:T(8,128)(2,1)} %v_hbm.1) | copy-start | bytes 98308
  5.3 0.7 %copy-start.4 = (bf16[64,128]{1,0:T(8,128)(2,1)S(1)}, bf16[64,128]{1,0:T(8,128)(2,1)}, u32[]{:S(2)}) copy-start(bf16[64,128]{1,0:T(8,128)(2,1)} %pk_hbm.1) | copy-start | bytes 49156
  6.0 0.7 %copy-start.5 = (bf16[64,128]{1,0:T(8,128)(2,1)S(1)}, bf16[64,128]{1,0:T(8,128)(2,1)}, u32[]{:S(2)}) copy-start(bf16[64,128]{1,0:T(8,128)(2,1)} %pv_hbm.1) | copy-start | bytes 49156
  6.7 0.7 %copy-start.6 = (s32[4]{0:T(128)S(1)}, s32[4]{0:T(128)}, u32[]{:S(2)}) copy-start(s32[4]{0:T(128)} %lengths_ref.1) | copy-start | bytes 52
  7.4 0.7 %copy-start.7 = (s32[4]{0:T(128)S(1)}, s32[4]{0:T(128)}, u32[]{:S(2)}) copy-start(s32[4]{0:T(128)} %groups_ref.1) | copy-start | bytes 52
  8.0 0.7 %copy-start.8 = (s32[128]{0:T(128)S(1)}, s32[128]{0:T(128)}, u32[]{:S(2)}) copy-start(s32[128]{0:T(128)} %param.12) | copy-start | bytes 1540

commit v2 on v1

--- a/solution.py
+++ b/solution.py
@@ -510,7 +510,7 @@
             dma((3,)),
         ],
         compiler_params=pltpu.CompilerParams(
-            collective_id=0, has_side_effects=True, vmem_limit_bytes=40 << 20
+            collective_id=0, has_side_effects=True, vmem_limit_bytes=60 << 20
         ),
     )(
         lengths,

time: 51.4 us -> 45 us (0.88)
  local copies, waits for them, and re-layouts: 8.7 us -> 1.67 us
  Pallas kernels: 41.6 us -> 42.5 us
    unnamed x19 -> x1, local copies, waits for them, and re-layouts: 8.7 us -> 1.67 us
    pallas_call x1, Pallas kernels: 41.6 us -> 42.5 us  [shards(): pl.pallas_call(functools.partial(fused_kernel, n), out_shape=jax.ShapeDty...]
where the time goes in v2:
time: 45 us; the launch traced here: 44.8 us
  Pallas kernels  42.5 us (94%)
  local copies, waits for them, and re-layouts  1.67 us (4%)
  between operations  0.66 us (1%)
    pallas_call x1, Pallas kernels, shards(): pl.pallas_call(functools.partial(fused_kernel, n), out_shape=jax.ShapeDty...  42.5 us
    unnamed x1, local copies, waits for them, and re-layouts  1.67 us

profile of v2, /device:TPU:0, one launch (start us, length us, event | category | flops | bytes accessed | tf_op | source)
XLA Modules:
  0.0 44.8 jit_solution(6114591235068922753)
XLA Ops:
  0.7 42.5 %shard_map.100 = bf16[128,1024]{1,0:T(8,128)(2,1)} custom-call(s32[4]{0:T(128)} %lengths_ref.1, s32[4]{0:T(128)} %groups_ref.1, s32[1]{0:T(128)S(6)} %copy.12.block_ref, s32[1,128]{1,0:T(1,128)} %bitcast.1, bf16[128,512]{1,0:T(8,128)(2,1)} %q_hbm.1, bf16[128,128]{1,0:T(8,128)(2,1)} %k_hbm.1, bf16[128,128]{1,0:T(8,128)(2,1)} %v_hbm.1, ...), custom_call_target="tpu_custom_call" | custom-call | tf_op jit(solution)/shard_map/pallas_call | solution.py:479
  43.2 1.7 %copy.13 = bf16[128,1024]{1,0:T(8,128)(2,1)} copy(bf16[128,1024]{1,0:T(8,128)(2,1)} %shard_map.100) | data formatting | bytes 524288

commit v3 on v2

--- a/solution.py
+++ b/solution.py
@@ -186,16 +186,13 @@
     q_buf,
     k_buf,
     v_buf,
-    pk_buf,
-    pv_buf,
     w_buf,
     meta_buf,
+    col_buf,
     score_buf,
     weight_buf,
     top_buf,
-    bias_buf,
     att_buf,
-    ret_buf,
     send_a,
     recv_a,
     send_b,
@@ -204,10 +201,13 @@
     recv_c,
     part_buf,
     local_sem,
-    own_sem,
     w_sem,
-    gather_send,
+    up_send,
+    down_send,
+    cross_send,
     gather_recv,
+    meta_send,
+    meta_recv,
     a2a_send,
     a2a_recv,
     red_send,
@@ -220,35 +220,43 @@
     c = m - y * 2
     sibling = y * 2 + (1 - c)
     across = (1 - y) * 2 + c
-    rows = q_buf.shape[0]
-    heads = q_buf.shape[1] // HEAD_WIDTH
+    rows = q_hbm.shape[0]
+    heads = q_hbm.shape[1] // HEAD_WIDTH
     piece = rows // n
     requests = lengths_ref.shape[0]
     per_group = n // GROUPS
     width = out_ref.shape[1]
-    peers = [lax.rem(me + k, n) for k in range(n)]
+    lines = n // 2
+    z = me // 2
+    x = me - z * 2
     MESH = pl.DeviceIdType.MESH
-
+    peers = [
+        lax.rem(z + lines - s // 2, lines) * 2 + (x if s % 2 == 0 else 1 - x) for s in range(n)
+    ]
+
+    local = [
+        pltpu.make_async_copy(k_hbm, k_buf.at[0, 0:rows], local_sem.at[0]),
+        pltpu.make_async_copy(pk_hbm, k_buf.at[0, rows:], local_sem.at[1]),
+        pltpu.make_async_copy(v_hbm, v_buf.at[0, 0:rows], local_sem.at[2]),
+        pltpu.make_async_copy(pv_hbm, v_buf.at[0, rows:], local_sem.at[3]),
+        pltpu.make_async_copy(
+            q_hbm.at[pl.ds(pl.multiple_of(me * piece, piece), piece)],
+            q_buf.at[0],
+            local_sem.at[4],
+        ),
+    ]
+    for copy in local:
+        copy.start()
     meta_buf[0] = jnp.zeros(meta_buf.shape[1:], jnp.int32)
     meta_buf[0, 0:1, :] = deal_ref[...]
     meta_buf[0, 1:2, :] = jnp.full((1, rows), block_ref[0] // per_group, jnp.int32)
 
     barrier = pltpu.get_barrier_semaphore()
-    for k in range(1, n):
-        pl.semaphore_signal(barrier, inc=1, device_id={"blk": peers[k]}, device_id_type=MESH)
+    for s in range(1, n):
+        pl.semaphore_signal(barrier, inc=1, device_id={"blk": peers[s]}, device_id_type=MESH)
     pl.semaphore_signal(barrier, inc=1, device_id={"mp": sibling}, device_id_type=MESH)
     pl.semaphore_signal(barrier, inc=1, device_id={"mp": across}, device_id_type=MESH)
-
-    local = [
-        pltpu.make_async_copy(q_hbm, q_buf, local_sem.at[0]),
-        pltpu.make_async_copy(k_hbm, k_buf.at[0], local_sem.at[1]),
-        pltpu.make_async_copy(v_hbm, v_buf.at[0], local_sem.at[2]),
-        pltpu.make_async_copy(pk_hbm, pk_buf.at[0], local_sem.at[3]),
-        pltpu.make_async_copy(pv_hbm, pv_buf.at[0], local_sem.at[4]),
-    ]
-    for copy in local:
-        copy.start()
-    order = [across_col for across_col in ((1 - y) * 2 + (1 - c), across, sibling, m)]
+    order = [(1 - y) * 2 + (1 - c), across, sibling, m]
     w_copies = [
         pltpu.make_async_copy(
             w_hbm.at[:, pl.ds(pl.multiple_of(order[i] * width, 128), width)],
@@ -257,39 +265,122 @@
         )
         for i in range(4)
     ]
+    for copy in local:
+        copy.wait()
     for copy in w_copies:
         copy.start()
     pl.semaphore_wait(barrier, n + 1)
 
-    def gather(k):
-        pairs = (
-            (meta_buf.at[0], meta_buf.at[k]),
-            (k_hbm, k_buf.at[k]),
-            (pk_hbm, pk_buf.at[k]),
-            (v_hbm, v_buf.at[k]),
-            (pv_hbm, pv_buf.at[k]),
-        )
-        return [
-            pltpu.make_async_remote_copy(
-                src_ref=source,
-                dst_ref=target,
-                send_sem=gather_send.at[k, i],
-                recv_sem=gather_recv.at[k, i],
-                device_id={"blk": peers[k]},
-                device_id_type=MESH,
-            )
-            for i, (source, target) in enumerate(pairs)
-        ]
-
-    gathers = [None] + [gather(k) for k in range(1, n)]
-    for i in range(5):
-        for k in range(1, n):
-            gathers[k][i].start()
+    bufs = (k_buf, v_buf)
+
+    def hop(part, source, target, device, sem):
+        return pltpu.make_async_remote_copy(
+            src_ref=bufs[part].at[source],
+            dst_ref=bufs[part].at[target],
+            send_sem=sem.at[source // 2, part],
+            recv_sem=gather_recv.at[target, part],
+            device_id={"blk": device},
+            device_id_type=MESH,
+        )
+
+    def up(part, r):
+        return hop(part, 2 * r, 2 * ((r + lines - 1) % lines), me + 2, up_send)
+
+    def down(part, r):
+        return hop(part, 2 * r, 2 * ((r + 1) % lines), me - 2, down_send)
+
+    def cross(part, r):
+        return hop(part, 2 * r, 2 * r + 1, z * 2 + 1 - x, cross_send)
+
+    def arrival(part, slot):
+        return hop(part, 0, slot, z * 2 + 1 - x, cross_send)
+
+    def forward(part, r, below, act):
+        if below:
+
+            @pl.when(z < lines - 1)
+            def _():
+                act(up(part, r))
+
+        else:
+
+            @pl.when(z > 0)
+            def _():
+                act(down(part, r))
+
+        act(cross(part, r))
+
+    def start(copy):
+        copy.start()
+
+    def ended(copy):
+        copy.wait_send()
+
+    queries_out = [None] + [
+        pltpu.make_async_remote_copy(
+            src_ref=q_hbm.at[pl.ds(pl.multiple_of(peers[s] * piece, piece), piece)],
+            dst_ref=q_buf.at[s],
+            send_sem=a2a_send.at[s],
+            recv_sem=a2a_recv.at[s],
+            device_id={"blk": peers[s]},
+            device_id_type=MESH,
+        )
+        for s in range(1, n)
+    ]
+    metas_out = [None] + [
+        pltpu.make_async_remote_copy(
+            src_ref=meta_buf.at[0],
+            dst_ref=meta_buf.at[s],
+            send_sem=meta_send.at[s],
+            recv_sem=meta_recv.at[s],
+            device_id={"blk": peers[s]},
+            device_id_type=MESH,
+        )
+        for s in range(1, n)
+    ]
+
+    def own(part, act):
+        @pl.when(z < lines - 1)
+        def _():
+            act(up(part, 0))
+
+        @pl.when(z > 0)
+        def _():
+            act(down(part, 0))
+
+        act(cross(part, 0))
+
+    own(0, start)
+    for s in range(1, n):
+        metas_out[s].start()
+    for s in range(1, n):
+        queries_out[s].start()
+    own(1, start)
+
+    def relay(distance):
+        for part in range(2):
+            for below in (True, False):
+                r = lines - distance if below else distance
+
+                @pl.when(z >= distance if below else z + distance < lines)
+                def _(part=part, below=below, r=r):
+                    arrival(part, 2 * r).wait_recv()
+                    forward(part, r, below, start)
 
     def column(row):
         return jnp.transpose(jnp.broadcast_to(row, (rows, rows)))
 
-    query_row = deal_ref[...]
+    relay(1)
+    lane = lax.broadcasted_iota(jnp.int32, (1, rows), 1)
+    query_row = jnp.zeros((1, rows), jnp.int32)
+    for s in range(n):
+        if s > 0:
+            metas_out[s].wait_recv()
+        shift = lax.rem((s + n - me) * piece, rows)
+        turned = pltpu.roll(meta_buf[s], shift, 1)[0:1, :]
+        query_row = jnp.where((lane >= s * piece) & (lane < (s + 1) * piece), turned, query_row)
+    target = lax.broadcasted_iota(jnp.int32, (rows, rows), 0)
+    select = jnp.where(target == query_row - me * rows, 1.0, 0.0).astype(jnp.bfloat16)
     start_row = jnp.zeros((1, rows), jnp.int32)
     group_row = jnp.full((1, rows), groups_ref[0], jnp.int32)
     end = lengths_ref[0]
@@ -298,51 +389,57 @@
         start_row = jnp.where(past, end, start_row)
         group_row = jnp.where(past, groups_ref[r], group_row)
         end = end + lengths_ref[r]
-    row_col = column(query_row)
-    start_col = column(start_row)
-    group_col = column(group_row)
-
-    for copy in local:
-        copy.wait()
+    col_buf[0] = column(query_row)
+    col_buf[1] = column(start_row)
+    col_buf[2] = column(group_row)
+    for s in range(1, n):
+        queries_out[s].wait_recv()
     scale = LOG2E / math.sqrt(HEAD_WIDTH)
-
-    def scored(h, keys, bias):
-        return (
-            lax.dot_general(
-                q_buf[:, h * HEAD_WIDTH : (h + 1) * HEAD_WIDTH],
-                keys,
-                (((1,), (1,)), ((), ())),
-                preferred_element_type=jnp.float32,
-            )
-            * scale
-            + bias
-        )
 
     def place(block, keys, bias, first):
         for h in range(heads):
-            scores = scored(h, keys, bias)
+            scores = (
+                lax.dot_general(
+                    q_buf[:, :, h * HEAD_WIDTH : (h + 1) * HEAD_WIDTH].reshape(rows, HEAD_WIDTH),
+                    keys,
+                    (((1,), (1,)), ((), ())),
+                    preferred_element_type=jnp.float32,
+                )
+                * scale
+                + bias
+            )
             score_buf[block, h] = scores
             if first:
                 top_buf[h] = scores
             else:
                 top_buf[h] = jnp.maximum(top_buf[h], scores)
 
-    lane = lax.broadcasted_iota(jnp.int32, (1, rows), 1)
-    for k in range(n):
-        if k > 0:
-            gathers[k][0].wait_recv()
-            gathers[k][1].wait_recv()
-        key_row = meta_buf[k, 0:1, :]
-        shown = (key_row >= start_col) & (key_row <= row_col)
-        bias = jnp.where(shown, 0.0, NEGATIVE)
-        place(k, k_buf[k], bias, k == 0)
-    for k in range(0, n, 2):
-        for j in (k, k + 1):
-            if j > 0:
-                gathers[j][2].wait_recv()
-        key_group = jnp.where(lane < rows // 2, meta_buf[k, 1:2, :], meta_buf[k + 1, 1:2, :])
-        bias = jnp.where(key_group == group_col, 0.0, NEGATIVE)
-        place(n + k // 2, pk_buf[k : k + 2].reshape(rows, HEAD_WIDTH), bias, False)
+    def score_pair(r):
+        arrival(0, 2 * r + 1).wait_recv()
+        for s in (2 * r, 2 * r + 1):
+            key_row = meta_buf[s, 0:1, :]
+            shown = (key_row >= col_buf[1]) & (key_row <= col_buf[0])
+            place(s, k_buf[s, 0:rows], jnp.where(shown, 0.0, NEGATIVE), s == 0)
+        key_group = jnp.where(
+            lane < rows // 2, meta_buf[2 * r, 1:2, :], meta_buf[2 * r + 1, 1:2, :]
+        )
+        bias = jnp.where(key_group == col_buf[2], 0.0, NEGATIVE)
+        place(
+            n + r, k_buf[2 * r : 2 * r + 2, rows:].reshape(rows, HEAD_WIDTH), bias, False
+        )
+
+    score_pair(0)
+    for distance in range(1, lines):
+        if distance + 1 < lines:
+            relay(distance + 1)
+
+        @pl.when(z >= distance)
+        def _(r=lines - distance):
+            score_pair(r)
+
+        @pl.when(z + distance < lines)
+        def _(r=distance):
+            score_pair(r)
 
     blocks = n + n // 2
     totals = []
@@ -356,50 +453,24 @@
                 jnp.bfloat16
             )
         totals.append(jnp.sum(total, axis=1, keepdims=True))
-    for k in range(1, n):
-        gathers[k][3].wait_recv()
-        gathers[k][4].wait_recv()
+    for r in range(lines):
+        arrival(1, 2 * r + 1).wait_recv()
     mixed = jnp.dot(
         weight_buf[:, : n * rows],
-        v_buf[...].reshape(n * rows, HEAD_WIDTH),
+        v_buf[:, 0:rows].reshape(n * rows, HEAD_WIDTH),
         preferred_element_type=jnp.float32,
     ) + jnp.dot(
         weight_buf[:, n * rows :],
-        pv_buf[...].reshape(n * rows // 2, HEAD_WIDTH),
+        v_buf[:, rows:].reshape(n * rows // 2, HEAD_WIDTH),
         preferred_element_type=jnp.float32,
     )
     for h in range(heads):
-        done = (mixed[h * rows : (h + 1) * rows] / totals[h]).astype(jnp.bfloat16)
-        att_buf[:, :, h * HEAD_WIDTH : (h + 1) * HEAD_WIDTH] = done.reshape(n, piece, HEAD_WIDTH)
-
-    returns = [None] + [
-        pltpu.make_async_remote_copy(
-            src_ref=att_buf.at[peers[k]],
-            dst_ref=ret_buf.at[k],
-            send_sem=a2a_send.at[k],
-            recv_sem=a2a_recv.at[k],
-            device_id={"blk": peers[k]},
-            device_id_type=MESH,
-        )
-        for k in range(1, n)
-    ]
-    for k in range(1, n):
-        returns[k].start()
-    ret_buf[0:1] = att_buf[pl.ds(me, 1)]
-
-    placed = jnp.zeros((1, rows), jnp.int32)
-    for k in range(n):
-        shift = lax.rem((k + n - me) * piece, rows)
-        turned = pltpu.roll(meta_buf[k], shift, 1)[0:1, :]
-        placed = jnp.where((lane >= k * piece) & (lane < (k + 1) * piece), turned, placed)
-    placed = placed - me * rows
-    target = lax.broadcasted_iota(jnp.int32, (rows, rows), 0)
-    select = jnp.where(target == placed, 1.0, 0.0).astype(jnp.bfloat16)
-    for k in range(1, n):
-        returns[k].wait_recv()
-    ordered = jnp.dot(
-        select, ret_buf[...].reshape(rows, -1), preferred_element_type=jnp.float32
-    ).astype(jnp.bfloat16)
+        att_buf[:, h * HEAD_WIDTH : (h + 1) * HEAD_WIDTH] = (
+            mixed[h * rows : (h + 1) * rows] / totals[h]
+        ).astype(jnp.bfloat16)
+    ordered = jnp.dot(select, att_buf[...], preferred_element_type=jnp.float32).astype(
+        jnp.bfloat16
+    )
 
     def reduce_copy(i, source, target, device):
         return pltpu.make_async_remote_copy(
@@ -431,10 +502,21 @@
     part_buf[...] = part_buf[...] + recv_c[...].astype(jnp.float32)
     copy_b.wait_recv()
     out_ref[...] = (part_buf[...] + recv_b[...].astype(jnp.float32)).astype(jnp.bfloat16)
-    for k in range(1, n):
-        for copy in gathers[k]:
-            copy.wait_send()
-        returns[k].wait_send()
+    for s in range(1, n):
+        metas_out[s].wait_send()
+        queries_out[s].wait_send()
+    for part in range(2):
+        own(part, ended)
+        for distance in range(1, lines):
+
+            @pl.when(z >= distance)
+            def _(part=part, r=lines - distance):
+                forward(part, r, True, ended)
+
+            @pl.when(z + distance < lines)
+            def _(part=part, r=distance):
+                forward(part, r, False, ended)
+
     for copy in (copy_a, copy_b, copy_c):
         copy.wait_send()
 
@@ -482,28 +564,28 @@
         in_specs=[smem, smem, smem, vmem, hbm, hbm, hbm, hbm, hbm, hbm],
         out_specs=vmem,
         scratch_shapes=[
-            pltpu.VMEM((rows, queries.shape[1]), bf16),
-            pltpu.VMEM((n, rows, HEAD_WIDTH), bf16),
-            pltpu.VMEM((n, rows, HEAD_WIDTH), bf16),
-            pltpu.VMEM((n, prefix_rows, HEAD_WIDTH), bf16),
-            pltpu.VMEM((n, prefix_rows, HEAD_WIDTH), bf16),
+            pltpu.VMEM((n, piece, queries.shape[1]), bf16),
+            pltpu.VMEM((n, rows + prefix_rows, HEAD_WIDTH), bf16),
+            pltpu.VMEM((n, rows + prefix_rows, HEAD_WIDTH), bf16),
             pltpu.VMEM((4, out_weight.shape[0], columns), bf16),
             pltpu.VMEM((n, 8, rows), jnp.int32),
+            pltpu.VMEM((3, rows, rows), jnp.int32),
             pltpu.VMEM((blocks, heads, rows, rows), f32),
             pltpu.VMEM((heads * rows, blocks * rows), bf16),
             pltpu.VMEM((heads, rows, rows), f32),
-            pltpu.VMEM((rows, rows), f32),
-            pltpu.VMEM((n, piece, heads * HEAD_WIDTH), bf16),
-            pltpu.VMEM((n, piece, heads * HEAD_WIDTH), bf16),
+            pltpu.VMEM((rows, heads * HEAD_WIDTH), bf16),
         ]
         + [pltpu.VMEM((rows, columns), bf16)] * 6
         + [
             pltpu.VMEM((rows, columns), f32),
             dma((5,)),
-            dma((1,)),
             dma((4,)),
-            dma((n, 5)),
-            dma((n, 5)),
+            dma((n // 2, 2)),
+            dma((n // 2, 2)),
+            dma((n // 2, 2)),
+            dma((n, 2)),
+            dma((n,)),
+            dma((n,)),
             dma((n,)),
             dma((n,)),
             dma((3,)),

time: 45 us -> 37.2 us (0.83)
  Pallas kernels: 42.5 us -> 34.6 us
    pallas_call x1, Pallas kernels: 42.5 us -> 34.6 us  [shards(): pl.pallas_call(functools.partial(fused_kernel, n), out_shape=jax.ShapeDty...]
where the time goes in v3:
time: 37.2 us; the launch traced here: 36.9 us
  Pallas kernels  34.6 us (93%)
  local copies, waits for them, and re-layouts  1.67 us (4%)
  between operations  0.66 us (2%)
    pallas_call x1, Pallas kernels, shards(): pl.pallas_call(functools.partial(fused_kernel, n), out_shape=jax.ShapeDty...  34.6 us
    unnamed x1, local copies, waits for them, and re-layouts  1.67 us

profile of v3, /device:TPU:0, one launch (start us, length us, event | category | flops | bytes accessed | tf_op | source)
XLA Modules:
  0.0 36.9 jit_solution(17798989407363187714)
XLA Ops:
  0.7 34.6 %shard_map.100 = bf16[128,1024]{1,0:T(8,128)(2,1)} custom-call(s32[4]{0:T(128)} %lengths_ref.1, s32[4]{0:T(128)} %groups_ref.1, s32[1]{0:T(128)S(6)} %copy.12.block_ref, s32[1,128]{1,0:T(1,128)} %bitcast.1, bf16[128,512]{1,0:T(8,128)(2,1)} %q_hbm.1, bf16[128,128]{1,0:T(8,128)(2,1)} %k_hbm.1, bf16[128,128]{1,0:T(8,128)(2,1)} %v_hbm.1, ...), custom_call_target="tpu_custom_call" | custom-call | tf_op jit(solution)/shard_map/pallas_call | solution.py:561
  35.3 1.7 %copy.13 = bf16[128,1024]{1,0:T(8,128)(2,1)} copy(bf16[128,1024]{1,0:T(8,128)(2,1)} %shard_map.100) | data formatting | bytes 524288

commit v4 on v3

--- a/solution.py
+++ b/solution.py
@@ -184,6 +184,7 @@
     w_hbm,
     out_ref,
     q_buf,
+    ordered_q,
     k_buf,
     v_buf,
     w_buf,
@@ -234,11 +235,17 @@
         lax.rem(z + lines - s // 2, lines) * 2 + (x if s % 2 == 0 else 1 - x) for s in range(n)
     ]
 
+    lead = 2 * piece
+    rest = lead + pk_hbm.shape[0]
+    held = rows + pk_hbm.shape[0]
+    window = pl.ds(pl.multiple_of((z // (lines - 1)) * lead, lead), held - lead)
     local = [
-        pltpu.make_async_copy(k_hbm, k_buf.at[0, 0:rows], local_sem.at[0]),
-        pltpu.make_async_copy(pk_hbm, k_buf.at[0, rows:], local_sem.at[1]),
-        pltpu.make_async_copy(v_hbm, v_buf.at[0, 0:rows], local_sem.at[2]),
-        pltpu.make_async_copy(pv_hbm, v_buf.at[0, rows:], local_sem.at[3]),
+        pltpu.make_async_copy(k_hbm.at[0:lead], k_buf.at[0, 0:lead], local_sem.at[0]),
+        pltpu.make_async_copy(pk_hbm, k_buf.at[0, lead:rest], local_sem.at[1]),
+        pltpu.make_async_copy(k_hbm.at[lead:], k_buf.at[0, rest:], local_sem.at[2]),
+        pltpu.make_async_copy(v_hbm.at[0:lead], v_buf.at[0, 0:lead], local_sem.at[3]),
+        pltpu.make_async_copy(pv_hbm, v_buf.at[0, lead:rest], local_sem.at[5]),
+        pltpu.make_async_copy(v_hbm.at[lead:], v_buf.at[0, rest:], local_sem.at[6]),
         pltpu.make_async_copy(
             q_hbm.at[pl.ds(pl.multiple_of(me * piece, piece), piece)],
             q_buf.at[0],
@@ -247,6 +254,10 @@
     ]
     for copy in local:
         copy.start()
+    for s in range(1, n, 2):
+        for buf in (k_buf, v_buf):
+            buf[s, 0:lead] = jnp.zeros((lead, HEAD_WIDTH), jnp.bfloat16)
+            buf[s, held - lead :] = jnp.zeros((lead, HEAD_WIDTH), jnp.bfloat16)
     meta_buf[0] = jnp.zeros(meta_buf.shape[1:], jnp.int32)
     meta_buf[0, 0:1, :] = deal_ref[...]
     meta_buf[0, 1:2, :] = jnp.full((1, rows), block_ref[0] // per_group, jnp.int32)
@@ -269,14 +280,29 @@
         copy.wait()
     for copy in w_copies:
         copy.start()
+    row_ids = lax.broadcasted_iota(jnp.int32, (rows, rows), 0) + me * rows
+    start_row = jnp.zeros((rows, rows), jnp.int32)
+    group_row = jnp.full((rows, rows), groups_ref[0], jnp.int32)
+    end = lengths_ref[0]
+    for r in range(1, requests):
+        past = row_ids >= end
+        start_row = jnp.where(past, end, start_row)
+        group_row = jnp.where(past, groups_ref[r], group_row)
+        end = end + lengths_ref[r]
+    col_buf[0] = row_ids
+    col_buf[1] = start_row
+    col_buf[2] = group_row
     pl.semaphore_wait(barrier, n + 1)
 
     bufs = (k_buf, v_buf)
 
     def hop(part, source, target, device, sem):
+        source_ref, target_ref = bufs[part].at[source], bufs[part].at[target]
+        if target % 2 == 1:
+            source_ref, target_ref = bufs[part].at[source, window], bufs[part].at[target, window]
         return pltpu.make_async_remote_copy(
-            src_ref=bufs[part].at[source],
-            dst_ref=bufs[part].at[target],
+            src_ref=source_ref,
+            dst_ref=target_ref,
             send_sem=sem.at[source // 2, part],
             recv_sem=gather_recv.at[target, part],
             device_id={"blk": device},
@@ -367,9 +393,6 @@
                     arrival(part, 2 * r).wait_recv()
                     forward(part, r, below, start)
 
-    def column(row):
-        return jnp.transpose(jnp.broadcast_to(row, (rows, rows)))
-
     relay(1)
     lane = lax.broadcasted_iota(jnp.int32, (1, rows), 1)
     query_row = jnp.zeros((1, rows), jnp.int32)
@@ -379,28 +402,19 @@
         shift = lax.rem((s + n - me) * piece, rows)
         turned = pltpu.roll(meta_buf[s], shift, 1)[0:1, :]
         query_row = jnp.where((lane >= s * piece) & (lane < (s + 1) * piece), turned, query_row)
-    target = lax.broadcasted_iota(jnp.int32, (rows, rows), 0)
-    select = jnp.where(target == query_row - me * rows, 1.0, 0.0).astype(jnp.bfloat16)
-    start_row = jnp.zeros((1, rows), jnp.int32)
-    group_row = jnp.full((1, rows), groups_ref[0], jnp.int32)
-    end = lengths_ref[0]
-    for r in range(1, requests):
-        past = query_row >= end
-        start_row = jnp.where(past, end, start_row)
-        group_row = jnp.where(past, groups_ref[r], group_row)
-        end = end + lengths_ref[r]
-    col_buf[0] = column(query_row)
-    col_buf[1] = column(start_row)
-    col_buf[2] = column(group_row)
+    select = jnp.where(col_buf[0] == query_row, 1.0, 0.0).astype(jnp.bfloat16)
     for s in range(1, n):
         queries_out[s].wait_recv()
+    ordered_q[...] = jnp.dot(
+        select, q_buf[...].reshape(rows, -1), preferred_element_type=jnp.float32
+    ).astype(jnp.bfloat16)
     scale = LOG2E / math.sqrt(HEAD_WIDTH)
 
     def place(block, keys, bias, first):
         for h in range(heads):
             scores = (
                 lax.dot_general(
-                    q_buf[:, :, h * HEAD_WIDTH : (h + 1) * HEAD_WIDTH].reshape(rows, HEAD_WIDTH),
+                    ordered_q[:, h * HEAD_WIDTH : (h + 1) * HEAD_WIDTH],
                     keys,
                     (((1,), (1,)), ((), ())),
                     preferred_element_type=jnp.float32,
@@ -419,13 +433,14 @@
         for s in (2 * r, 2 * r + 1):
             key_row = meta_buf[s, 0:1, :]
             shown = (key_row >= col_buf[1]) & (key_row <= col_buf[0])
-            place(s, k_buf[s, 0:rows], jnp.where(shown, 0.0, NEGATIVE), s == 0)
+            suffix = jnp.concatenate([k_buf[s, 0:lead], k_buf[s, rest:]], axis=0)
+            place(s, suffix, jnp.where(shown, 0.0, NEGATIVE), s == 0)
         key_group = jnp.where(
             lane < rows // 2, meta_buf[2 * r, 1:2, :], meta_buf[2 * r + 1, 1:2, :]
         )
         bias = jnp.where(key_group == col_buf[2], 0.0, NEGATIVE)
         place(
-            n + r, k_buf[2 * r : 2 * r + 2, rows:].reshape(rows, HEAD_WIDTH), bias, False
+            n + r, k_buf[2 * r : 2 * r + 2, lead:rest].reshape(rows, HEAD_WIDTH), bias, False
         )
 
     score_pair(0)
@@ -442,35 +457,38 @@
             score_pair(r)
 
     blocks = n + n // 2
-    totals = []
-    for h in range(heads):
-        top = jnp.max(top_buf[h], axis=1, keepdims=True)
-        total = jnp.zeros((rows, rows), jnp.float32)
-        for b in range(blocks):
-            weights = jnp.exp2(score_buf[b, h] - top)
-            total = total + weights
-            weight_buf[h * rows : (h + 1) * rows, b * rows : (b + 1) * rows] = weights.astype(
-                jnp.bfloat16
-            )
-        totals.append(jnp.sum(total, axis=1, keepdims=True))
-    for r in range(lines):
-        arrival(1, 2 * r + 1).wait_recv()
-    mixed = jnp.dot(
-        weight_buf[:, : n * rows],
-        v_buf[:, 0:rows].reshape(n * rows, HEAD_WIDTH),
-        preferred_element_type=jnp.float32,
-    ) + jnp.dot(
-        weight_buf[:, n * rows :],
-        v_buf[:, rows:].reshape(n * rows // 2, HEAD_WIDTH),
-        preferred_element_type=jnp.float32,
-    )
-    for h in range(heads):
-        att_buf[:, h * HEAD_WIDTH : (h + 1) * HEAD_WIDTH] = (
-            mixed[h * rows : (h + 1) * rows] / totals[h]
-        ).astype(jnp.bfloat16)
-    ordered = jnp.dot(select, att_buf[...], preferred_element_type=jnp.float32).astype(
-        jnp.bfloat16
-    )
+    half = rows // 2
+
+    def attention(i):
+        part = slice(i * half, (i + 1) * half)
+        totals = []
+        for h in range(heads):
+            top = jnp.max(top_buf[h, part], axis=1, keepdims=True)
+            total = jnp.zeros((half, rows), jnp.float32)
+            for b in range(blocks):
+                weights = jnp.exp2(score_buf[b, h, part] - top)
+                total = total + weights
+                weight_buf[i, h * half : (h + 1) * half, b * rows : (b + 1) * rows] = (
+                    weights.astype(jnp.bfloat16)
+                )
+            totals.append(jnp.sum(total, axis=1, keepdims=True))
+        if i == 0:
+            for r in range(lines):
+                arrival(1, 2 * r + 1).wait_recv()
+        suffix = jnp.concatenate([v_buf[:, 0:lead], v_buf[:, rest:]], axis=1)
+        mixed = jnp.dot(
+            weight_buf[i, :, : n * rows],
+            suffix.reshape(n * rows, HEAD_WIDTH),
+            preferred_element_type=jnp.float32,
+        ) + jnp.dot(
+            weight_buf[i, :, n * rows :],
+            v_buf[:, lead:rest].reshape(n * rows // 2, HEAD_WIDTH),
+            preferred_element_type=jnp.float32,
+        )
+        for h in range(heads):
+            att_buf[part, h * HEAD_WIDTH : (h + 1) * HEAD_WIDTH] = (
+                mixed[h * half : (h + 1) * half] / totals[h]
+            ).astype(jnp.bfloat16)
 
     def reduce_copy(i, source, target, device):
         return pltpu.make_async_remote_copy(
@@ -482,26 +500,39 @@
             device_id_type=MESH,
         )
 
-    def project(i):
-        w_copies[i].wait()
-        return jnp.dot(ordered, w_buf[i], preferred_element_type=jnp.float32)
-
-    copy_a = reduce_copy(0, send_a, recv_a, sibling)
-    copy_b = reduce_copy(1, send_b, recv_b, across)
-    copy_c = reduce_copy(2, send_c, recv_c, sibling)
-    send_a[...] = project(0).astype(jnp.bfloat16)
-    copy_a.start()
-    part_buf[...] = project(1)
-    copy_a.wait_recv()
-    send_b[...] = (part_buf[...] + recv_a[...].astype(jnp.float32)).astype(jnp.bfloat16)
-    copy_b.start()
-    send_c[...] = project(2).astype(jnp.bfloat16)
+    def project(i, part):
+        return jnp.dot(att_buf[part], w_buf[i], preferred_element_type=jnp.float32)
+
+    halves = [slice(i * half, (i + 1) * half) for i in range(2)]
+    copies_a = [
+        reduce_copy(i, send_a.at[p], recv_a.at[p], sibling) for i, p in enumerate(halves)
+    ]
+    copies_b = [
+        reduce_copy(2 + i, send_b.at[p], recv_b.at[p], across) for i, p in enumerate(halves)
+    ]
+    copy_c = reduce_copy(4, send_c, recv_c, sibling)
+    for i, p in enumerate(halves):
+        attention(i)
+        if i == 0:
+            w_copies[0].wait()
+        send_a[p] = project(0, p).astype(jnp.bfloat16)
+        copies_a[i].start()
+        if i == 0:
+            w_copies[1].wait()
+        part_buf[p] = project(1, p)
+        copies_a[i].wait_recv()
+        send_b[p] = (part_buf[p] + recv_a[p].astype(jnp.float32)).astype(jnp.bfloat16)
+        copies_b[i].start()
+    w_copies[2].wait()
+    send_c[...] = project(2, slice(0, rows)).astype(jnp.bfloat16)
     copy_c.start()
-    part_buf[...] = project(3)
+    w_copies[3].wait()
+    part_buf[...] = project(3, slice(0, rows))
     copy_c.wait_recv()
     part_buf[...] = part_buf[...] + recv_c[...].astype(jnp.float32)
-    copy_b.wait_recv()
-    out_ref[...] = (part_buf[...] + recv_b[...].astype(jnp.float32)).astype(jnp.bfloat16)
+    for copy, p in zip(copies_b, halves):
+        copy.wait_recv()
+        out_ref[p] = (part_buf[p] + recv_b[p].astype(jnp.float32)).astype(jnp.bfloat16)
     for s in range(1, n):
         metas_out[s].wait_send()
         queries_out[s].wait_send()
@@ -517,7 +548,7 @@
             def _(part=part, r=distance):
                 forward(part, r, False, ended)
 
-    for copy in (copy_a, copy_b, copy_c):
+    for copy in copies_a + copies_b + [copy_c]:
         copy.wait_send()
 
 
@@ -536,7 +567,7 @@
     n = lax.axis_size("blk")
     rows = queries.shape[0]
     piece = rows // n
-    if piece % 16 != 0 or rows != 128 or 2 * prefix_key_blocks.shape[0] != rows:
+    if n != 8 or rows != 128 or 2 * prefix_key_blocks.shape[0] != rows:
         return plain_shards(
             lengths,
             groups,
@@ -565,20 +596,21 @@
         out_specs=vmem,
         scratch_shapes=[
             pltpu.VMEM((n, piece, queries.shape[1]), bf16),
+            pltpu.VMEM((rows, queries.shape[1]), bf16),
             pltpu.VMEM((n, rows + prefix_rows, HEAD_WIDTH), bf16),
             pltpu.VMEM((n, rows + prefix_rows, HEAD_WIDTH), bf16),
             pltpu.VMEM((4, out_weight.shape[0], columns), bf16),
             pltpu.VMEM((n, 8, rows), jnp.int32),
             pltpu.VMEM((3, rows, rows), jnp.int32),
             pltpu.VMEM((blocks, heads, rows, rows), f32),
-            pltpu.VMEM((heads * rows, blocks * rows), bf16),
+            pltpu.VMEM((2, heads * rows // 2, blocks * rows), bf16),
             pltpu.VMEM((heads, rows, rows), f32),
             pltpu.VMEM((rows, heads * HEAD_WIDTH), bf16),
         ]
         + [pltpu.VMEM((rows, columns), bf16)] * 6
         + [
             pltpu.VMEM((rows, columns), f32),
-            dma((5,)),
+            dma((7,)),
             dma((4,)),
             dma((n // 2, 2)),
             dma((n // 2, 2)),
@@ -588,8 +620,8 @@
             dma((n,)),
             dma((n,)),
             dma((n,)),
-            dma((3,)),
-            dma((3,)),
+            dma((5,)),
+            dma((5,)),
         ],
         compiler_params=pltpu.CompilerParams(
             collective_id=0, has_side_effects=True, vmem_limit_bytes=60 << 20

time: 37.2 us -> 36.5 us (0.981)
  Pallas kernels: 34.6 us -> 33.9 us
    pallas_call x1, Pallas kernels: 34.6 us -> 33.9 us  [shards(): pl.pallas_call(functools.partial(fused_kernel, n), out_shape=jax.ShapeDty...]
where the time goes in v4:
time: 36.5 us; the launch traced here: 36.2 us
  Pallas kernels  33.9 us (93%)
  local copies, waits for them, and re-layouts  1.67 us (5%)
  between operations  0.66 us (2%)
    pallas_call x1, Pallas kernels, shards(): pl.pallas_call(functools.partial(fused_kernel, n), out_shape=jax.ShapeDty...  33.9 us
    unnamed x1, local copies, waits for them, and re-layouts  1.67 us

profile of v4, /device:TPU:0, one launch (start us, length us, event | category | flops | bytes accessed | tf_op | source)
XLA Modules:
  0.0 36.2 jit_solution(11588130354425985)
XLA Ops:
  0.7 33.9 %shard_map.100 = bf16[128,1024]{1,0:T(8,128)(2,1)} custom-call(s32[4]{0:T(128)} %lengths_ref.1, s32[4]{0:T(128)} %groups_ref.1, s32[1]{0:T(128)S(6)} %copy.12.block_ref, s32[1,128]{1,0:T(1,128)} %bitcast.1, bf16[128,512]{1,0:T(8,128)(2,1)} %q_hbm.1, bf16[128,128]{1,0:T(8,128)(2,1)} %k_hbm.1, bf16[128,128]{1,0:T(8,128)(2,1)} %v_hbm.1, ...), custom_call_target="tpu_custom_call" | custom-call | tf_op jit(solution)/shard_map/pallas_call | solution.py:592
  34.5 1.7 %copy.13 = bf16[128,1024]{1,0:T(8,128)(2,1)} copy(bf16[128,1024]{1,0:T(8,128)(2,1)} %shard_map.100) | data formatting | bytes 524288

commit v5 on v4

--- a/solution.py
+++ b/solution.py
@@ -235,10 +235,14 @@
         lax.rem(z + lines - s // 2, lines) * 2 + (x if s % 2 == 0 else 1 - x) for s in range(n)
     ]
 
-    lead = 2 * piece
+    lead = 3 * piece
     rest = lead + pk_hbm.shape[0]
     held = rows + pk_hbm.shape[0]
-    window = pl.ds(pl.multiple_of((z // (lines - 1)) * lead, lead), held - lead)
+
+    def window(block):
+        first = jnp.maximum(block - n // 2, 0) * piece
+        return pl.ds(pl.multiple_of(first, piece), held - lead)
+
     local = [
         pltpu.make_async_copy(k_hbm.at[0:lead], k_buf.at[0, 0:lead], local_sem.at[0]),
         pltpu.make_async_copy(pk_hbm, k_buf.at[0, lead:rest], local_sem.at[1]),
@@ -299,7 +303,9 @@
     def hop(part, source, target, device, sem):
         source_ref, target_ref = bufs[part].at[source], bufs[part].at[target]
         if target % 2 == 1:
-            source_ref, target_ref = bufs[part].at[source, window], bufs[part].at[target, window]
+            seen = window(me if sem is None else device)
+            source_ref, target_ref = bufs[part].at[source, seen], bufs[part].at[target, seen]
+            sem = cross_send
         return pltpu.make_async_remote_copy(
             src_ref=source_ref,
             dst_ref=target_ref,
@@ -319,7 +325,7 @@
         return hop(part, 2 * r, 2 * r + 1, z * 2 + 1 - x, cross_send)
 
     def arrival(part, slot):
-        return hop(part, 0, slot, z * 2 + 1 - x, cross_send)
+        return hop(part, 0, slot, z * 2 + 1 - x, None if slot % 2 == 1 else cross_send)
 
     def forward(part, r, below, act):
         if below:
@@ -377,11 +383,11 @@
         act(cross(part, 0))
 
     own(0, start)
+    own(1, start)
     for s in range(1, n):
         metas_out[s].start()
     for s in range(1, n):
         queries_out[s].start()
-    own(1, start)
 
     def relay(distance):
         for part in range(2):

time: 36.5 us -> 35.1 us (0.962)
  Pallas kernels: 33.9 us -> 32.4 us
    pallas_call x1, Pallas kernels: 33.9 us -> 32.4 us  [shards(): pl.pallas_call(functools.partial(fused_kernel, n), out_shape=jax.ShapeDty...]
where the time goes in v5:
time: 35.1 us; the launch traced here: 34.7 us
  Pallas kernels  32.4 us (92%)
  local copies, waits for them, and re-layouts  1.67 us (5%)
  between operations  0.66 us (2%)
    pallas_call x1, Pallas kernels, shards(): pl.pallas_call(functools.partial(fused_kernel, n), out_shape=jax.ShapeDty...  32.4 us
    unnamed x1, local copies, waits for them, and re-layouts  1.67 us

profile of v5, /device:TPU:0, one launch (start us, length us, event | category | flops | bytes accessed | tf_op | source)
XLA Modules:
  0.0 34.7 jit_solution(15891325544411733569)
XLA Ops:
  0.7 32.4 %shard_map.100 = bf16[128,1024]{1,0:T(8,128)(2,1)} custom-call(s32[4]{0:T(128)} %lengths_ref.1, s32[4]{0:T(128)} %groups_ref.1, s32[1]{0:T(128)S(6)} %copy.12.block_ref, s32[1,128]{1,0:T(1,128)} %bitcast.1, bf16[128,512]{1,0:T(8,128)(2,1)} %q_hbm.1, bf16[128,128]{1,0:T(8,128)(2,1)} %k_hbm.1, bf16[128,128]{1,0:T(8,128)(2,1)} %v_hbm.1, ...), custom_call_target="tpu_custom_call" | custom-call | tf_op jit(solution)/shard_map/pallas_call | solution.py:598
  33.1 1.7 %copy.13 = bf16[128,1024]{1,0:T(8,128)(2,1)} copy(bf16[128,1024]{1,0:T(8,128)(2,1)} %shard_map.100) | data formatting | bytes 524288

commit v6 on v5

--- a/solution.py
+++ b/solution.py
@@ -400,6 +400,7 @@
                     forward(part, r, below, start)
 
     relay(1)
+    relay(2)
     lane = lax.broadcasted_iota(jnp.int32, (1, rows), 1)
     query_row = jnp.zeros((1, rows), jnp.int32)
     for s in range(n):
@@ -451,7 +452,7 @@
 
     score_pair(0)
     for distance in range(1, lines):
-        if distance + 1 < lines:
+        if 2 < distance + 1 < lines:
             relay(distance + 1)
 
         @pl.when(z >= distance)

time: 35.1 us -> 34.7 us (0.989)
    pallas_call x1, Pallas kernels: 32.4 us -> 32.1 us  [shards(): pl.pallas_call(functools.partial(fused_kernel, n), out_shape=jax.ShapeDty...]
where the time goes in v6:
time: 34.7 us; the launch traced here: 34.4 us
  Pallas kernels  32.1 us (93%)
  local copies, waits for them, and re-layouts  1.67 us (5%)
  between operations  0.66 us (2%)
    pallas_call x1, Pallas kernels, shards(): pl.pallas_call(functools.partial(fused_kernel, n), out_shape=jax.ShapeDty...  32.1 us
    unnamed x1, local copies, waits for them, and re-layouts  1.67 us

profile of v6, /device:TPU:0, one launch (start us, length us, event | category | flops | bytes accessed | tf_op | source)
XLA Modules:
  0.0 34.4 jit_solution(5482222614608997673)
XLA Ops:
  0.7 32.1 %shard_map.100 = bf16[128,1024]{1,0:T(8,128)(2,1)} custom-call(s32[4]{0:T(128)} %lengths_ref.1, s32[4]{0:T(128)} %groups_ref.1, s32[1]{0:T(128)S(6)} %copy.12.block_ref, s32[1,128]{1,0:T(1,128)} %bitcast.1, bf16[128,512]{1,0:T(8,128)(2,1)} %q_hbm.1, bf16[128,128]{1,0:T(8,128)(2,1)} %k_hbm.1, bf16[128,128]{1,0:T(8,128)(2,1)} %v_hbm.1, ...), custom_call_target="tpu_custom_call" | custom-call | tf_op jit(solution)/shard_map/pallas_call | solution.py:599
  32.7 1.7 %copy.13 = bf16[128,1024]{1,0:T(8,128)(2,1)} copy(bf16[128,1024]{1,0:T(8,128)(2,1)} %shard_map.100) | data formatting | bytes 524288
